TPU v7x, 32 devices: a whole 2x2x4 slice. The times are simulated.
32 devices in a mesh: groups: 2 (over x), dap: 16 (over z, y, core).
Axes of the slice: x: 2, y: 2, z: 4, core: 2. Of those that a mesh axis runs over, the one named last changes fastest.
Arguments:
- homolog_tensor: bfloat16 [128, 32, 256], P(('groups', 'dap')), parts along dimension 0, may hold values from -1 to 1
- couple_tensor: bfloat16 [64, 32, 128], P(('groups', 'dap')), parts along dimension 0, may hold values from -6 to 6
- horizontal_drop_filter: int32 [64, 256], P('groups'), parts along dimension 0, may hold values 0 or 1
- couple_offset_matrix: bfloat16 [128, 8], replicated, may hold values from -0.29882812 to 0.29882812
- horizontal_attend_matrix: bfloat16 [256, 1024], replicated, may hold values from -0.375 to 0.375
- horizontal_exit_matrix: bfloat16 [256, 256], replicated, may hold values from -0.375 to 0.375
- vertical_attend_matrix: bfloat16 [256, 1024], replicated, may hold values from -0.375 to 0.375
- vertical_exit_matrix: bfloat16 [256, 256], replicated, may hold values from -0.375 to 0.375
- averaged_product_flanks: bfloat16 [256, 64], replicated, may hold values from -0.375 to 0.375
- averaged_product_exit: bfloat16 [1024, 128], replicated, may hold values from -1 to 1
Outputs:
- alignment_output: bfloat16 [128, 32, 256], P('groups', 'dap'), parts along dimension 0
- pair_output_state: bfloat16 [64, 32, 128], P(('groups', 'dap')), parts along dimension 0
There are 2 independent parts, one for each index of `groups`. A program takes and returns all parts, laid end to end along the dimension named above; an argument that names none is the same for every part. Nothing has to cross between parts.
All inputs are finite; a program needn't handle non-finite values.
Results may differ from a plain program's by a relative error of at most 0.012.
Values may be sent and summed in bfloat16 or wider, within the bound.
No kernel may reach another device: no remote copies, remote signals or barrier semaphores. Data moves between devices by JAX's collectives and lax.ppermute only.
A program may use at most 64 MiB of HBM per device.

v0:
```python
import jax
import jax.numpy as jnp
from jax import lax
from jax.sharding import PartitionSpec as P

HEAD_NUMBER = 8
HEAD_WIDTH = 32
FACTOR_FEATURES = 32


def standardise_features(values):
    values = values.astype(jnp.float32)
    center = values - jnp.mean(values, axis=-1, keepdims=True)
    spread = jnp.mean(center * center, axis=-1, keepdims=True)
    return center * lax.rsqrt(spread + 1e-05)


def attend(normed, w_qkvg, w_out, bias):
    batch, length = (normed.shape[0], normed.shape[1])
    proj = jnp.einsum("blc,cf->blf", normed, w_qkvg, preferred_element_type=jnp.float32)
    proj = proj.reshape(batch, length, 4, HEAD_NUMBER, HEAD_WIDTH)
    query = (proj[:, :, 0] * HEAD_WIDTH ** (-0.5)).astype(jnp.bfloat16)
    keys = proj[:, :, 1].astype(jnp.bfloat16)
    values = proj[:, :, 2].astype(jnp.bfloat16)
    gate = proj[:, :, 3]
    if bias is None:
        bias = jnp.zeros((HEAD_NUMBER, length, length), jnp.bfloat16)

    def one_head(items):
        qh, kh, vh, bh = items
        scores = jnp.einsum("bid,bjd->bij", qh, kh, preferred_element_type=jnp.float32)
        scores = scores + bh.astype(jnp.float32)[None]
        weights = jax.nn.softmax(scores, axis=-1).astype(jnp.bfloat16)
        return jnp.einsum("bij,bjd->bid", weights, vh, preferred_element_type=jnp.float32)

    heads = lax.map(
        one_head,
        (jnp.moveaxis(query, 2, 0), jnp.moveaxis(keys, 2, 0), jnp.moveaxis(values, 2, 0), bias),
    )
    heads = jnp.moveaxis(heads, 0, 2)
    gated = (
        (jax.nn.sigmoid(gate) * heads)
        .astype(jnp.bfloat16)
        .reshape(batch, length, HEAD_NUMBER * HEAD_WIDTH)
    )
    return jnp.einsum("blk,kc->blc", gated, w_out, preferred_element_type=jnp.float32)


def shards(
    homolog_tensor,
    couple_tensor,
    horizontal_drop_filter,
    couple_offset_matrix,
    horizontal_attend_matrix,
    horizontal_exit_matrix,
    vertical_attend_matrix,
    vertical_exit_matrix,
    averaged_product_flanks,
    averaged_product_exit,
):
    normed_pair = standardise_features(couple_tensor).astype(jnp.bfloat16)
    own_bias = jnp.einsum(
        "ijz,zh->hij", normed_pair, couple_offset_matrix, preferred_element_type=jnp.float32
    ).astype(jnp.bfloat16)
    bias = lax.all_gather(own_bias, "dap", axis=1, tiled=True)
    starting_answer = standardise_features(homolog_tensor).astype(jnp.bfloat16)
    perform_refresh = attend(
        starting_answer, horizontal_attend_matrix, horizontal_exit_matrix, bias
    )
    homolog_later = (
        homolog_tensor.astype(jnp.float32)
        + horizontal_drop_filter.astype(jnp.float32) * (1.0 / 0.9) * perform_refresh
    ).astype(jnp.bfloat16)
    incoming_blocks = lax.all_to_all(homolog_later, "dap", split_axis=1, concat_axis=0, tiled=True)
    column_layout = jnp.swapaxes(incoming_blocks, 0, 1)
    perform_refresh = attend(
        standardise_features(column_layout).astype(jnp.bfloat16),
        vertical_attend_matrix,
        vertical_exit_matrix,
        None,
    )
    alignment_output = jnp.swapaxes(
        (column_layout.astype(jnp.float32) + perform_refresh).astype(jnp.bfloat16), 0, 1
    )
    final_result = standardise_features(alignment_output).astype(jnp.bfloat16)
    factors = jnp.einsum(
        "sic,cf->sif", final_result, averaged_product_flanks, preferred_element_type=jnp.float32
    )
    left = factors[..., :FACTOR_FEATURES].astype(jnp.bfloat16)
    right = factors[..., FACTOR_FEATURES:].astype(jnp.bfloat16)
    total = left.shape[0]
    own_rows = left.shape[1]
    whole = lax.all_gather(right, "dap", axis=1, tiled=True)
    outer = jnp.einsum("sic,sjd->ijcd", left, whole, preferred_element_type=jnp.float32) / total
    outer = outer.astype(jnp.bfloat16).reshape(
        own_rows, whole.shape[1], FACTOR_FEATURES * FACTOR_FEATURES
    )
    change = jnp.einsum(
        "ijk,kz->ijz", outer, averaged_product_exit, preferred_element_type=jnp.float32
    )
    pair_output_state = (couple_tensor.astype(jnp.float32) + change).astype(jnp.bfloat16)
    return (alignment_output, pair_output_state)


def solution(mesh):
    placed = (
        P(("groups", "dap"), None, None),
        P(("groups", "dap"), None, None),
        P("groups", None),
        P(),
        P(),
        P(),
        P(),
        P(),
        P(),
        P(),
    )
    return jax.shard_map(
        shards,
        mesh=mesh,
        in_specs=placed,
        out_specs=(P("groups", "dap", None), P(("groups", "dap"), None, None)),
        check_vma=False,
    )
```

profile of v0, /device:TPU:0, one launch (start us, length us, event | category | flops | bytes accessed | tf_op | source)
XLA Modules:
  0.0 80.2 jit_solution(14656866743398978957)
XLA Ops:
  0.6 1.0 %convert_reduce_fusion = f32[4,32]{1,0:T(4,128)S(1)} fusion(bf16[4,32,256]{2,1,0:T(8,128)(2,1)} %param.14), kind=kLoop, calls=%fused_computation.81 | loop fusion | flops 65408 | bytes 66048 | tf_op jit(solution)/shard_map/reduce_sum | solution.py:13
  1.7 1.0 %fusion.104 = f32[4,32]{1,0:T(4,128)S(1)} fusion(bf16[4,32,256]{2,1,0:T(8,128)(2,1)} %param.14, f32[4,32]{1,0:T(4,128)S(1)} %broadcast_multiply_fusion), kind=kLoop, calls=%fused_computation.88 | loop fusion | flops 130944 | bytes 66560 | tf_op jit(solution)/shard_map/reduce_sum | solution.py:14
  2.7 1.1 %fusion.87 = f32[4,32,1024]{2,1,0:T(8,128)S(1)} fusion(bf16[256,1024]{1,0:T(8,128)(2,1)S(1)} %copy-done, bf16[4,32,256]{2,1,0:T(8,128)(2,1)} %param.14, f32[4,32]{1,0:T(4,128)S(1)} %add_rsqrt_fusion, f32[4,32]{1,0:T(4,128)S(1)} %broadcast_multiply_fusion), kind=kOutput, calls=%fused_computation.63 | convolution fusion | flops 67239936 | bytes 1115136 | tf_op jit(solution)/shard_map/blc,cf->blf/dot_general | solution.py:20
  3.8 0.7 reshape.102
  4.5 2.6 %copy.41 = f32[4,32,4,8,32]{4,1,0,3,2:T(8,128)} copy(f32[4,32,4,8,32]{4,3,2,1,0:T(8,128)S(1)} %reshape.102) | data formatting | bytes 1048576 | tf_op jit(solution)/shard_map/reshape | solution.py:21
  7.1 2.2 %copy.76 = bf16[4,32,4,8,32]{4,1,0,3,2:T(8,128)(2,1)} copy(f32[4,32,4,8,32]{4,3,2,1,0:T(8,128)S(1)} %reshape.102) | data formatting | bytes 786432 | tf_op jit(solution)/shard_map/reshape | solution.py:21
  9.3 1.1 %fusion.90 = bf16[8,4,32,32]{3,2,1,0:T(8,128)(2,1)S(1)} fusion(f32[4,32,4,8,32]{4,1,0,3,2:T(8,128)} %copy.41), kind=kLoop, calls=%fused_computation.66 | loop fusion | flops 65536 | bytes 196608 | tf_op jit(solution)/shard_map/transpose | solution.py:38
  10.4 1.1 %slice_bitcast_fusion = (bf16[8,4,32,32]{3,2,1,0:T(8,128)(2,1)S(1)}, bf16[8,4,32,32]{3,2,1,0:T(8,128)(2,1)S(1)}) fusion(bf16[4,32,4,8,32]{4,1,0,3,2:T(8,128)(2,1)} %copy.76), kind=kLoop, calls=%fused_computation.75 | loop fusion | bytes 262144 | tf_op jit(solution)/shard_map/transpose | solution.py:38
  11.9 23.3 %all_gather.6 = bf16[8,32,32]{2,0,1:T(8,128)(2,1)S(1)} all-gather(bf16[8,2,32]{2,0,1:T(8,128)(2,1)S(1)} %fusion.78), channel_id=1, replica_groups=mesh['groups'=2,'dap'=16] {'dap'}, dimensions={1}, use_global_device_ids=true | all-gather | bytes 17408 | tf_op jit(solution)/shard_map/all_gather | solution.py:65
  35.4 4.3 %while.20 = (s32[]{:T(128)}, f32[8,4,32,32]{3,2,1,0:T(8,128)S(1)}, bf16[8,4,32,32]{3,2,1,0:T(8,128)(2,1)S(1)}, bf16[8,4,32,32]{3,2,1,0:T(8,128)(2,1)S(1)}, bf16[...) while((s32[]{:T(128)}, f32[8,4,32,32]{3,2,1,0:T(8,128)S(1)}, ...), condition=%wide.region_7.8_spmd, body=%wide.region_4.7_spmd.sunk | while | flops 816320 | bytes 274001 | solution.py:36
  35.6 0.3 fusion.162
  36.1 0.3 fusion.162
  38.8 0.3 fusion.162
  39.3 0.3 fusion.162
  39.7 1.3 %fusion.89 = bf16[4,32,8,32]{3,1,0,2:T(8,128)(2,1)S(1)} fusion(f32[8,4,32,32]{3,2,1,0:T(8,128)S(1)} %get-tuple-element.61, f32[4,32,4,8,32]{4,1,0,3,2:T(8,128)} %copy.41), kind=kLoop, calls=%fused_computation.65 | loop fusion | flops 163840 | bytes 327680 | tf_op jit(solution)/shard_map/convert_element_type | solution.py:43
  41.5 0.7 copy.46
  42.2 3.5 %all-to-all-start = ((bf16[4,32,256]{2,0,1:T(4,128)(2,1)}), bf16[4,32,256]{2,0,1:T(4,128)(2,1)S(1)}, u32[]{:S(2)}, u32[]{:S(2)}) async-start(bf16[4,32,256]{2,0,1:T(4,128)(2,1)} %copy.46), calls=%async_computation | async-start | bytes 131072 | tf_op jit(solution)/shard_map/all_to_all | solution.py:74
  45.7 6.8 %all-to-all-done = bf16[4,32,256]{2,0,1:T(4,128)(2,1)S(1)} async-done(((bf16[4,32,256]{2,0,1:T(4,128)(2,1)}), bf16[4,32,256]{2,0,1:T(4,128)(2,1)S(1)}, u32[]{:S(2)}, u32[]{:S(2)}) %all-to-all-start) | async-done | bytes 65568 | tf_op jit(solution)/shard_map/all_to_all | solution.py:74
  52.9 0.4 fusion.85
  53.5 4.7 %while.21 = (s32[]{:T(128)}, f32[8,2,64,32]{2,3,0,1:T(8,128)S(1)}, bf16[8,2,64,32]{2,3,0,1:T(8,128)(2,1)S(1)}, bf16[8,2,64,32]{2,3,0,1:T(8,128)(2,1)S(1)}, bf16[8,2,64,32]{2,3,0,1:T(8,128)(2,1)S(1)}, /*index=5*/s32[]{:T(128)}) while((s32[]{:T(128)}, f32[8,2,64,32]{2,3,0,1:T(8,128)S(1)}, bf16[8,2,64,32]{2,3,0,1:T(8,128)(2,1)S(1)}, ...), condition=%wide.region_13.14_spmd, body=%wide.region_10.13_spmd.sunk | while | flops 1614080 | bytes 119365 | solution.py:36
  53.8 0.3 fusion.169
  54.4 0.3 fusion.169
  55.0 0.3 fusion.169
  55.6 0.3 fusion.169
  56.1 0.3 fusion.169
  56.7 0.3 fusion.169
  57.3 0.3 fusion.169
  57.9 0.3 fusion.169
  58.7 0.7 copy.55
  59.8 18.5 %all_gather.7 = bf16[64,32,32]{0,2,1:T(8,128)(2,1)S(1)} all-gather(bf16[64,2,32]{0,2,1:T(8,128)(2,1)S(1)} %slice.54), channel_id=1, replica_groups=mesh['groups'=2,'dap'=16] {'dap'}, dimensions={1}, use_global_device_ids=true | all-gather | bytes 139264 | tf_op jit(solution)/shard_map/all_gather | solution.py:93
  78.9 0.5 reshape.106
  79.5 0.8 fusion.77
  (80 shorter events, 7.8 us)
Async XLA Ops:
  0.6 2.0 %copy-start = (bf16[256,1024]{1,0:T(8,128)(2,1)S(1)}, bf16[256,1024]{1,0:T(8,128)(2,1)}, u32[]{:S(2)}) copy-start(bf16[256,1024]{1,0:T(8,128)(2,1)} %param.18) | copy-start | bytes 1572868
  7.1 4.4 %copy-start.4 = (bf16[2,32,128]{2,1,0:T(8,128)(2,1)S(1)}, bf16[2,32,128]{2,1,0:T(8,128)(2,1)}, u32[]{:S(2)}) copy-start(bf16[2,32,128]{2,1,0:T(8,128)(2,1)} %param.15) | copy-start | bytes 49156
  7.1 4.7 %copy-start.9 = (bf16[128,8]{0,1:T(8,128)(2,1)S(1)}, bf16[128,8]{0,1:T(8,128)(2,1)}, u32[]{:S(2)}) copy-start(bf16[128,8]{0,1:T(8,128)(2,1)} %param.17) | copy-start | bytes 6148
  35.4 5.9 %copy-start.7 = (s32[32,256]{1,0:T(8,128)S(1)}, s32[32,256]{1,0:T(8,128)}, u32[]{:S(2)}) copy-start(s32[32,256]{1,0:T(8,128)} %param.16) | copy-start | bytes 98308
  35.4 5.9 %copy-start.1 = (bf16[4,32,256]{2,1,0:T(8,128)(2,1)S(1)}, bf16[4,32,256]{2,1,0:T(8,128)(2,1)}, u32[]{:S(2)}) copy-start(bf16[4,32,256]{2,1,0:T(8,128)(2,1)} %param.14) | copy-start | bytes 196612
  35.4 5.9 %copy-start.6 = (bf16[256,256]{1,0:T(8,128)(2,1)S(1)}, bf16[256,256]{1,0:T(8,128)(2,1)}, u32[]{:S(2)}) copy-start(bf16[256,256]{1,0:T(8,128)(2,1)} %param.19) | copy-start | bytes 393220
  39.7 13.2 %copy-start.2 = (bf16[256,1024]{1,0:T(8,128)(2,1)S(1)}, bf16[256,1024]{1,0:T(8,128)(2,1)}, u32[]{:S(2)}) copy-start(bf16[256,1024]{1,0:T(8,128)(2,1)} %param.20) | copy-start | bytes 1572868
  42.2 10.4 %all-to-all-start = ((bf16[4,32,256]{2,0,1:T(4,128)(2,1)}), bf16[4,32,256]{2,0,1:T(4,128)(2,1)S(1)}, u32[]{:S(2)}, u32[]{:S(2)}) async-start(bf16[4,32,256]{2,0,1:T(4,128)(2,1)} %copy.46), calls=%async_computation | async-start | bytes 131072 | tf_op jit(solution)/shard_map/all_to_all | solution.py:74
  53.4 4.9 %copy-start.5 = (bf16[256,256]{1,0:T(8,128)(2,1)S(1)}, bf16[256,256]{1,0:T(8,128)(2,1)}, u32[]{:S(2)}) copy-start(bf16[256,256]{1,0:T(8,128)(2,1)} %param.21) | copy-start | bytes 393220
  53.5 6.1 %copy-start.8 = (bf16[256,64]{0,1:T(8,128)(2,1)S(1)}, bf16[256,64]{0,1:T(8,128)(2,1)}, u32[]{:S(2)}) copy-start(bf16[256,64]{0,1:T(8,128)(2,1)} %param.22) | copy-start | bytes 98308
  58.3 21.2 %copy-start.3 = (bf16[1024,128]{1,0:T(8,128)(2,1)S(1)}, bf16[1024,128]{1,0:T(8,128)(2,1)}, u32[]{:S(2)}) copy-start(bf16[1024,128]{1,0:T(8,128)(2,1)} %param.23) | copy-start | bytes 786436
where the time goes:
time: 80.6 us; the launch traced here: 80.2 us
  blocking collectives  41.8 us (52%)
  matrix products  12.4 us (15%)
  local copies, waits for them, and re-layouts  9.33 us (12%)
  waiting for transfers between devices  6.85 us (8%)
  other arithmetic  5.33 us (7%)
  starting transfers between devices  3.5 us (4%)
  between operations  0.95 us (1%)
    all_gather x1, blocking collectives, shards(): bias = lax.all_gather(own_bias, 'dap', axis=1, tiled=True)  23.3 us
    all_gather x1, blocking collectives, shards(): whole = lax.all_gather(right, 'dap', axis=1, tiled=True)  18.5 us
    all_to_all x1, waiting for transfers between devices, shards(): lax.all_to_all(homolog_later, 'dap', split_axis=1, concat_axis=0, tiled=T...  6.85 us
    dot_general x16, matrix products, one_head(): jnp.einsum('bij,bjd->bid', weights, vh, preferred_element_type=jnp.float32)  5.53 us
    reshape x3, local copies, waits for them, and re-layouts, attend(): proj = proj.reshape(batch, length, 4, HEAD_NUMBER, HEAD_WIDTH)  5.46 us
    all_to_all x1, starting transfers between devices, shards(): lax.all_to_all(homolog_later, 'dap', split_axis=1, concat_axis=0, tiled=T...  3.5 us
    sub x16, matrix products, one_head(): weights = jax.nn.softmax(scores, axis=-1).astype(jnp.bfloat16)  3.4 us
  transfers between devices with their start and end apart: 1, of which 1 were waited for; matrix products, arithmetic and copies ran while one was open for 0% of the time, Pallas kernels for 0%

commit v1 on v0

--- a/solution.py
+++ b/solution.py
@@ -90,7 +90,15 @@
     right = factors[..., FACTOR_FEATURES:].astype(jnp.bfloat16)
     total = left.shape[0]
     own_rows = left.shape[1]
-    whole = lax.all_gather(right, "dap", axis=1, tiled=True)
+    whole = jnp.concatenate(
+        lax.all_to_all(
+            jnp.stack([right for _ in range(lax.psum(1, axis_name="dap"))], 0),
+            "dap",
+            split_axis=0,
+            concat_axis=0,
+        ),
+        1,
+    )
     outer = jnp.einsum("sic,sjd->ijcd", left, whole, preferred_element_type=jnp.float32) / total
     outer = outer.astype(jnp.bfloat16).reshape(
         own_rows, whole.shape[1], FACTOR_FEATURES * FACTOR_FEATURES

time: 80.6 us -> 74.1 us (0.919)
  blocking collectives: 41.8 us -> 23.3 us
  waiting for transfers between devices: 6.85 us -> 14 us
  starting transfers between devices: 3.5 us -> 7.01 us
  local copies, waits for them, and re-layouts: 9.33 us -> 10.5 us
    all_gather x1 -> x0, blocking collectives: 18.5 us -> none  [shards(): whole = lax.all_gather(right, 'dap', axis=1, tiled=True)]
    all_to_all x0 -> x1, waiting for transfers between devices: none -> 7.17 us  [shards(): lax.all_to_all(jnp.stack([right for _ in range(lax.psum(1, axis_name='dap...]
    all_to_all x0 -> x1, starting transfers between devices: none -> 3.51 us  [shards(): lax.all_to_all(jnp.stack([right for _ in range(lax.psum(1, axis_name='dap...]
    unnamed x21 -> x24, local copies, waits for them, and re-layouts: 0.76 us -> 1.89 us
  transfers between devices with their start and end apart: 1 -> 2, of which waited for: 1 -> 2; matrix products, arithmetic and copies ran while one was open for 0% -> 1% of each run, Pallas kernels for 0% -> 0%
where the time goes in v1:
time: 74.1 us; the launch traced here: 73.6 us
  blocking collectives  23.3 us (31%)
  waiting for transfers between devices  14 us (19%)
  matrix products  12.4 us (17%)
  local copies, waits for them, and re-layouts  10.5 us (14%)
  starting transfers between devices  7.01 us (9%)
  other arithmetic  5.33 us (7%)
  between operations  0.99 us (1%)
    all_gather x1, blocking collectives, shards(): bias = lax.all_gather(own_bias, 'dap', axis=1, tiled=True)  23.3 us
    all_to_all x1, waiting for transfers between devices, shards(): lax.all_to_all(jnp.stack([right for _ in range(lax.psum(1, axis_name='dap...  7.17 us
    all_to_all x1, waiting for transfers between devices, shards(): lax.all_to_all(homolog_later, 'dap', split_axis=1, concat_axis=0, tiled=T...  6.85 us
    dot_general x16, matrix products, one_head(): jnp.einsum('bij,bjd->bid', weights, vh, preferred_element_type=jnp.float32)  5.53 us
    reshape x3, local copies, waits for them, and re-layouts, attend(): proj = proj.reshape(batch, length, 4, HEAD_NUMBER, HEAD_WIDTH)  5.46 us
    all_to_all x1, starting transfers between devices, shards(): lax.all_to_all(jnp.stack([right for _ in range(lax.psum(1, axis_name='dap...  3.51 us
    all_to_all x1, starting transfers between devices, shards(): lax.all_to_all(homolog_later, 'dap', split_axis=1, concat_axis=0, tiled=T...  3.5 us
    sub x16, matrix products, one_head(): weights = jax.nn.softmax(scores, axis=-1).astype(jnp.bfloat16)  3.4 us
  transfers between devices with their start and end apart: 2, of which 2 were waited for; matrix products, arithmetic and copies ran while one was open for 1% of the time, Pallas kernels for 0%

profile of v1, /device:TPU:0, one launch (start us, length us, event | category | flops | bytes accessed | tf_op | source)
XLA Modules:
  0.0 73.6 jit_solution(13600373186008178615)
XLA Ops:
  0.6 1.0 %convert_reduce_fusion = f32[4,32]{1,0:T(4,128)S(1)} fusion(bf16[4,32,256]{2,1,0:T(8,128)(2,1)} %param.14), kind=kLoop, calls=%fused_computation.80 | loop fusion | flops 65408 | bytes 66048 | tf_op jit(solution)/shard_map/reduce_sum | solution.py:13
  1.7 1.0 %fusion.103 = f32[4,32]{1,0:T(4,128)S(1)} fusion(bf16[4,32,256]{2,1,0:T(8,128)(2,1)} %param.14, f32[4,32]{1,0:T(4,128)S(1)} %broadcast_multiply_fusion), kind=kLoop, calls=%fused_computation.87 | loop fusion | flops 130944 | bytes 66560 | tf_op jit(solution)/shard_map/reduce_sum | solution.py:14
  2.7 1.1 %fusion.87 = f32[4,32,1024]{2,1,0:T(8,128)S(1)} fusion(bf16[256,1024]{1,0:T(8,128)(2,1)S(1)} %copy-done, bf16[4,32,256]{2,1,0:T(8,128)(2,1)} %param.14, f32[4,32]{1,0:T(4,128)S(1)} %add_rsqrt_fusion, f32[4,32]{1,0:T(4,128)S(1)} %broadcast_multiply_fusion), kind=kOutput, calls=%fused_computation.63 | convolution fusion | flops 67239936 | bytes 1115136 | tf_op jit(solution)/shard_map/blc,cf->blf/dot_general | solution.py:20
  3.8 0.7 reshape.110
  4.5 2.6 %copy.41 = f32[4,32,4,8,32]{4,1,0,3,2:T(8,128)} copy(f32[4,32,4,8,32]{4,3,2,1,0:T(8,128)S(1)} %reshape.110) | data formatting | bytes 1048576 | tf_op jit(solution)/shard_map/reshape | solution.py:21
  7.1 2.2 %copy.76 = bf16[4,32,4,8,32]{4,1,0,3,2:T(8,128)(2,1)} copy(f32[4,32,4,8,32]{4,3,2,1,0:T(8,128)S(1)} %reshape.110) | data formatting | bytes 786432 | tf_op jit(solution)/shard_map/reshape | solution.py:21
  9.3 1.1 %fusion.90 = bf16[8,4,32,32]{3,2,1,0:T(8,128)(2,1)S(1)} fusion(f32[4,32,4,8,32]{4,1,0,3,2:T(8,128)} %copy.41), kind=kLoop, calls=%fused_computation.66 | loop fusion | flops 65536 | bytes 196608 | tf_op jit(solution)/shard_map/transpose | solution.py:38
  10.4 1.1 %slice_bitcast_fusion = (bf16[8,4,32,32]{3,2,1,0:T(8,128)(2,1)S(1)}, bf16[8,4,32,32]{3,2,1,0:T(8,128)(2,1)S(1)}) fusion(bf16[4,32,4,8,32]{4,1,0,3,2:T(8,128)(2,1)} %copy.76), kind=kLoop, calls=%fused_computation.75 | loop fusion | bytes 262144 | tf_op jit(solution)/shard_map/transpose | solution.py:38
  11.9 23.3 %all_gather.3 = bf16[8,32,32]{2,0,1:T(8,128)(2,1)S(1)} all-gather(bf16[8,2,32]{2,0,1:T(8,128)(2,1)S(1)} %fusion.78), channel_id=1, replica_groups=mesh['groups'=2,'dap'=16] {'dap'}, dimensions={1}, use_global_device_ids=true | all-gather | bytes 17408 | tf_op jit(solution)/shard_map/all_gather | solution.py:65
  35.4 4.3 %while.20 = (s32[]{:T(128)}, f32[8,4,32,32]{3,2,1,0:T(8,128)S(1)}, bf16[8,4,32,32]{3,2,1,0:T(8,128)(2,1)S(1)}, bf16[8,4,32,32]{3,2,1,0:T(8,128)(2,1)S(1)}, bf16[...) while((s32[]{:T(128)}, f32[8,4,32,32]{3,2,1,0:T(8,128)S(1)}, ...), condition=%wide.region_7.8_spmd, body=%wide.region_4.7_spmd.sunk | while | flops 816320 | bytes 274001 | solution.py:36
  38.8 0.3 fusion.162
  39.3 0.3 fusion.162
  39.7 1.3 %fusion.89 = bf16[4,32,8,32]{3,1,0,2:T(8,128)(2,1)S(1)} fusion(f32[8,4,32,32]{3,2,1,0:T(8,128)S(1)} %get-tuple-element.61, f32[4,32,4,8,32]{4,1,0,3,2:T(8,128)} %copy.41), kind=kLoop, calls=%fused_computation.65 | loop fusion | flops 163840 | bytes 327680 | tf_op jit(solution)/shard_map/convert_element_type | solution.py:43
  41.5 0.7 copy.46
  42.2 3.5 %all-to-all-start = ((bf16[4,32,256]{2,0,1:T(4,128)(2,1)}), bf16[4,32,256]{2,0,1:T(4,128)(2,1)S(1)}, u32[]{:S(2)}, u32[]{:S(2)}) async-start(bf16[4,32,256]{2,0,1:T(4,128)(2,1)} %copy.46), calls=%async_computation | async-start | bytes 131072 | tf_op jit(solution)/shard_map/all_to_all | solution.py:74
  45.7 6.8 %all-to-all-done = bf16[4,32,256]{2,0,1:T(4,128)(2,1)S(1)} async-done(((bf16[4,32,256]{2,0,1:T(4,128)(2,1)}), bf16[4,32,256]{2,0,1:T(4,128)(2,1)S(1)}, u32[]{:S(2)}, u32[]{:S(2)}) %all-to-all-start) | async-done | bytes 65568 | tf_op jit(solution)/shard_map/all_to_all | solution.py:74
  52.9 0.4 fusion.85
  53.5 4.7 %while.21 = (s32[]{:T(128)}, f32[8,2,64,32]{2,3,0,1:T(8,128)S(1)}, bf16[8,2,64,32]{2,3,0,1:T(8,128)(2,1)S(1)}, bf16[8,2,64,32]{2,3,0,1:T(8,128)(2,1)S(1)}, bf16[8,2,64,32]{2,3,0,1:T(8,128)(2,1)S(1)}, /*index=5*/s32[]{:T(128)}) while((s32[]{:T(128)}, f32[8,2,64,32]{2,3,0,1:T(8,128)S(1)}, bf16[8,2,64,32]{2,3,0,1:T(8,128)(2,1)S(1)}, ...), condition=%wide.region_13.14_spmd, body=%wide.region_10.13_spmd.sunk | while | flops 1614080 | bytes 119365 | solution.py:36
  53.8 0.3 fusion.169
  54.4 0.3 fusion.169
  55.0 0.3 fusion.169
  55.6 0.3 fusion.169
  56.1 0.3 fusion.169
  56.7 0.3 fusion.169
  57.3 0.3 fusion.169
  57.9 0.3 fusion.169
  59.2 0.9 %reshape.131 = bf16[16,2,2048]{2,1,0:T(2,128)(2,1)} reshape(bf16[16,2,32,64]{3,2,1,0:T(8,128)(2,1)S(1)} %broadcast_bitcast_fusion) | data formatting | bytes 262144
  60.1 3.5 %all-to-all-start.1 = ((bf16[16,2,2048]{2,1,0:T(2,128)(2,1)}), bf16[16,2,2048]{2,1,0:T(2,128)(2,1)S(1)}, u32[]{:S(2)}, u32[]{:S(2)}) async-start(bf16[16,2,2048]{2,1,0:T(2,128)(2,1)} %reshape.131), calls=%async_computation.1 | async-start | bytes 262144 | tf_op jit(solution)/shard_map/all_to_all | solution.py:94
  63.6 0.7 copy.55
  64.3 7.2 %all-to-all-done.1 = bf16[16,2,2048]{2,1,0:T(2,128)(2,1)S(1)} async-done(((bf16[16,2,2048]{2,1,0:T(2,128)(2,1)}), bf16[16,2,2048]{2,1,0:T(2,128)(2,1)S(1)}, u32[]{:S(2)}, u32[]{:S(2)}) %all-to-all-start.1) | async-done | bytes 131104 | tf_op jit(solution)/shard_map/all_to_all | solution.py:94
  72.3 0.5 reshape.116
  72.8 0.8 %fusion.77 = bf16[2,32,128]{2,1,0:T(8,128)(2,1)} fusion(bf16[2,32,1024]{2,1,0:T(8,128)(2,1)S(1)} %reshape.116, bf16[1024,128]{1,0:T(8,128)(2,1)S(1)} %copy-done.3, bf16[2,32,128]{2,1,0:T(8,128)(2,1)S(1)} %copy-done.4), kind=kOutput, calls=%fused_computation.50 | convolution fusion | flops 16801792 | bytes 425984 | tf_op jit(solution)/shard_map/ijk,kz->ijz/dot_general | solution.py:106
  (84 shorter events, 8.8 us)
Async XLA Ops:
  0.6 2.0 %copy-start = (bf16[256,1024]{1,0:T(8,128)(2,1)S(1)}, bf16[256,1024]{1,0:T(8,128)(2,1)}, u32[]{:S(2)}) copy-start(bf16[256,1024]{1,0:T(8,128)(2,1)} %param.18) | copy-start | bytes 1572868
  7.1 4.4 %copy-start.4 = (bf16[2,32,128]{2,1,0:T(8,128)(2,1)S(1)}, bf16[2,32,128]{2,1,0:T(8,128)(2,1)}, u32[]{:S(2)}) copy-start(bf16[2,32,128]{2,1,0:T(8,128)(2,1)} %param.15) | copy-start | bytes 49156
  7.1 4.7 %copy-start.9 = (bf16[128,8]{0,1:T(8,128)(2,1)S(1)}, bf16[128,8]{0,1:T(8,128)(2,1)}, u32[]{:S(2)}) copy-start(bf16[128,8]{0,1:T(8,128)(2,1)} %param.17) | copy-start | bytes 6148
  35.4 5.9 %copy-start.7 = (s32[32,256]{1,0:T(8,128)S(1)}, s32[32,256]{1,0:T(8,128)}, u32[]{:S(2)}) copy-start(s32[32,256]{1,0:T(8,128)} %param.16) | copy-start | bytes 98308
  35.4 5.9 %copy-start.1 = (bf16[4,32,256]{2,1,0:T(8,128)(2,1)S(1)}, bf16[4,32,256]{2,1,0:T(8,128)(2,1)}, u32[]{:S(2)}) copy-start(bf16[4,32,256]{2,1,0:T(8,128)(2,1)} %param.14) | copy-start | bytes 196612
  35.4 5.9 %copy-start.6 = (bf16[256,256]{1,0:T(8,128)(2,1)S(1)}, bf16[256,256]{1,0:T(8,128)(2,1)}, u32[]{:S(2)}) copy-start(bf16[256,256]{1,0:T(8,128)(2,1)} %param.19) | copy-start | bytes 393220
  39.7 13.2 %copy-start.2 = (bf16[256,1024]{1,0:T(8,128)(2,1)S(1)}, bf16[256,1024]{1,0:T(8,128)(2,1)}, u32[]{:S(2)}) copy-start(bf16[256,1024]{1,0:T(8,128)(2,1)} %param.20) | copy-start | bytes 1572868
  42.2 10.4 %all-to-all-start = ((bf16[4,32,256]{2,0,1:T(4,128)(2,1)}), bf16[4,32,256]{2,0,1:T(4,128)(2,1)S(1)}, u32[]{:S(2)}, u32[]{:S(2)}) async-start(bf16[4,32,256]{2,0,1:T(4,128)(2,1)} %copy.46), calls=%async_computation | async-start | bytes 131072 | tf_op jit(solution)/shard_map/all_to_all | solution.py:74
  53.4 4.9 %copy-start.5 = (bf16[256,256]{1,0:T(8,128)(2,1)S(1)}, bf16[256,256]{1,0:T(8,128)(2,1)}, u32[]{:S(2)}) copy-start(bf16[256,256]{1,0:T(8,128)(2,1)} %param.21) | copy-start | bytes 393220
  53.4 5.4 %copy-start.8 = (bf16[256,64]{0,1:T(8,128)(2,1)S(1)}, bf16[256,64]{0,1:T(8,128)(2,1)}, u32[]{:S(2)}) copy-start(bf16[256,64]{0,1:T(8,128)(2,1)} %param.22) | copy-start | bytes 98308
  58.8 14.0 %copy-start.3 = (bf16[1024,128]{1,0:T(8,128)(2,1)S(1)}, bf16[1024,128]{1,0:T(8,128)(2,1)}, u32[]{:S(2)}) copy-start(bf16[1024,128]{1,0:T(8,128)(2,1)} %param.23) | copy-start | bytes 786436
  60.1 11.4 %all-to-all-start.1 = ((bf16[16,2,2048]{2,1,0:T(2,128)(2,1)}), bf16[16,2,2048]{2,1,0:T(2,128)(2,1)S(1)}, u32[]{:S(2)}, u32[]{:S(2)}) async-start(bf16[16,2,2048]{2,1,0:T(2,128)(2,1)} %reshape.131), calls=%async_computation.1 | async-start | bytes 262144 | tf_op jit(solution)/shard_map/all_to_all | solution.py:94
